TPU v7x, 32 devices: a whole 2x2x4 slice. The times are simulated.
32 devices in a mesh: groups: 2 (over y), head: 4 (over z), hist: 4 (over x, core).
Axes of the slice: x: 2, y: 2, z: 4, core: 2. Of those that a mesh axis runs over, the one named last changes fastest.
Arguments:
- tokens: bfloat16 [1024, 8192], P('groups', 'hist'), parts along dimension 0, may hold values from -6 to 6
- w_qkvu: bfloat16 [8192, 4, 8192], P('hist', None, 'head'), may hold values from -0.0625 to 0.0625
- k_cache: bfloat16 [4096, 8192], P(('groups', 'hist'), 'head'), parts along dimension 0, may hold values from -6 to 6
- v_cache: bfloat16 [4096, 8192], P(('groups', 'hist'), 'head'), parts along dimension 0
- w_out: bfloat16 [8192, 8192], P('head', 'hist'), may hold values from -0.0625 to 0.0625
- vis_start: int32 [1024], P('groups'), parts along dimension 0, may hold values from 0 to 511, as said below
- vis_end: int32 [1024], P('groups'), parts along dimension 0, may hold values from 1025 to 2048
Outputs:
- layer_out: bfloat16 [1024, 8192], P(('groups', 'head'), 'hist'), parts along dimension 0
There are 2 independent parts, one for each index of `groups`. A program takes and returns all parts, laid end to end along the dimension named above; an argument that names none is the same for every part. Nothing has to cross between parts.
Inputs may be any that keep to these rules, and one draw needn't show every extreme that they name: vis_start and vis_end together leave every candidate 2048 // 4 + 2 or more visible history events.
All inputs are finite; a program needn't handle non-finite values.
Results may differ from a plain program's by a relative error of at most 0.02.
Values may be sent and summed in bfloat16 or wider, within the bound.
A program may use at most 192 MiB of HBM per device.

v0:
```python
import jax
import jax.numpy as jnp
from jax import lax
from jax.sharding import PartitionSpec as P

DH = 128
epsilon = 1e-05


def history_terms(query_heads, key_block, value_block, vis_lo, vis_hi):
    head_total = query_heads.shape[1]
    head_size = query_heads.shape[2]
    block_len = key_block.shape[0]
    key_heads = key_block.reshape(block_len, head_total, head_size)
    value_heads = value_block.reshape(block_len, head_total, head_size)
    scores = jnp.einsum(
        "rhe,lhe->rhl", query_heads, key_heads, preferred_element_type=jnp.float32
    ) * head_size ** (-0.5)
    positions = lax.iota(jnp.int32, block_len)
    visible = (positions[None, :] >= vis_lo[:, None]) & (positions[None, :] < vis_hi[:, None])
    weights = jnp.where(visible[:, None, :], jax.nn.silu(scores), 0.0).astype(jnp.bfloat16)
    summed_values = jnp.einsum(
        "rhl,lhe->rhe", weights, value_heads, preferred_element_type=jnp.float32
    )
    return summed_values.reshape(query_heads.shape[0], head_total * head_size)


def local(tokens, w_qkvu, k_cache, v_cache, w_out, vis_start, vis_end):
    cand_total = tokens.shape[0]
    hist_count = lax.axis_size("hist")
    head_count = lax.axis_size("head")
    own_count = cand_total // hist_count
    own_first = lax.axis_index("hist") * own_count
    local_width = w_qkvu.shape[2]
    local_heads = local_width // DH
    full_width = local_width * head_count
    flat_weight = w_qkvu.reshape(w_qkvu.shape[0], 4 * local_width)
    start_own = lax.dynamic_slice_in_dim(vis_start, own_first, own_count)
    end_own = lax.dynamic_slice_in_dim(vis_end, own_first, own_count)
    summed = lax.psum_scatter(
        jnp.dot(tokens, flat_weight, preferred_element_type=jnp.float32).astype(jnp.bfloat16),
        "hist",
        scatter_dimension=0,
        tiled=True,
    ).astype(jnp.float32)
    own_part = jax.nn.silu(summed).astype(jnp.bfloat16).reshape(own_count, 4, local_width)
    own_query = own_part[:, 0]
    own_key = own_part[:, 1]
    own_value = own_part[:, 2]
    own_gate = own_part[:, 3]
    query_heads = own_query.reshape(own_count, local_heads, DH)
    history = history_terms(
        query_heads,
        lax.all_gather(k_cache, "hist", axis=0, tiled=True),
        lax.all_gather(v_cache, "hist", axis=0, tiled=True),
        start_own,
        end_own,
    )
    counts = (end_own - start_own).astype(jnp.float32)
    own_product = own_query.astype(jnp.float32) * own_key.astype(jnp.float32)
    own_score = jnp.sum(own_product.reshape(own_count, local_heads, DH), axis=2) * DH ** (-0.5)
    own_term = jax.nn.silu(own_score)[:, :, None] * own_value.astype(jnp.float32).reshape(
        own_count, local_heads, DH
    )
    attended = history / jnp.sqrt(counts)[:, None] + own_term.reshape(own_count, local_width)
    row_sum = lax.psum(jnp.sum(attended, axis=1), "head")
    centered = attended - (row_sum / full_width)[:, None]
    spread = lax.psum(jnp.sum(centered * centered, axis=1), "head")
    normed = centered * lax.rsqrt(spread / full_width + epsilon)[:, None]
    gated_rows = (normed * own_gate.astype(jnp.float32)).astype(jnp.bfloat16)
    gathered = lax.all_gather(gated_rows, "hist", axis=0, tiled=True)
    out_count = cand_total // head_count
    out_first = lax.axis_index("head") * out_count
    whole_out = jnp.dot(gathered, w_out, preferred_element_type=jnp.float32)
    total_out = lax.psum(whole_out.astype(jnp.bfloat16), "head").astype(jnp.float32)
    summed_out = lax.dynamic_slice_in_dim(total_out, out_first, out_count, 0)
    residual = lax.dynamic_slice_in_dim(tokens, out_first, out_count, 0).astype(jnp.float32)
    return (residual + summed_out).astype(jnp.bfloat16)


def solution(mesh):
    in_specs = (
        P("groups", "hist"),
        P("hist", None, "head"),
        P(("groups", "hist"), "head"),
        P(("groups", "hist"), "head"),
        P("head", "hist"),
        P("groups"),
        P("groups"),
    )
    out_specs = P(("groups", "head"), "hist")
    return jax.shard_map(local, mesh=mesh, in_specs=in_specs, out_specs=out_specs, check_vma=False)
```

profile of v0, /device:TPU:0, one launch (start us, length us, event | category | flops | bytes accessed | tf_op | source)
XLA Modules:
  0.0 367.3 jit_solution(18409414456210205719)
XLA Ops:
  6.5 0.0 all-gather.6.cloned.1.call-start
  6.5 0.7 all-gather.6.cloned.1.call-update
  7.3 0.0 reduce-scatter.2.cloned.1.call-start
  7.3 0.0 copy-start.2
  7.3 30.2 %copy.29 = bf16[256,8,4,2048]{3,1,2,0:T(8,128)(2,1)} copy(bf16[256,8,4,2048]{3,2,1,0:T(4,128)(2,1)} %bitcast.58) | data formatting | bytes 67108864
  37.5 0.0 copy-done.2
  37.5 25.5 %convolution_convert_fusion = bf16[512,8192]{1,0:T(8,128)(2,1)} fusion(bf16[512,2048]{1,0:T(8,128)(2,1)S(1)} %copy-done.2, bf16[2048,8192]{1,0:T(8,128)(2,1)} %bitcast.59), kind=kOutput, calls=%fused_computation.7 | convolution fusion | flops 17184063488 | bytes 44040192 | tf_op jit(solution)/shard_map/dot_general | solution.py:41
  63.0 0.0 copy-start.1
  63.0 0.0 reduce-scatter.2.cloned.1.call-update
  63.0 0.0 all-gather.4.cloned.1.call-start
  63.1 1.6 copy-done.1
  64.7 2.5 copy.14
  67.2 0.0 all-gather.4.cloned.1.call-update
  67.3 0.2 all-gather.8.cloned.1.call-start
  67.5 0.8 convert_sqrt_fusion
  68.3 0.5 fusion.19
  68.8 1.1 all-gather.6.cloned.1.call-done
  69.9 12.4 %copy.17 = bf16[2048,2048]{0,1:T(8,128)(2,1)} copy(bf16[2048,2048]{1,0:T(8,128)(2,1)} %all-gather.6.cloned.1.call-done) | data formatting | bytes 16777216 | tf_op jit(solution)/shard_map/all_gather | solution.py:55
  82.3 61.6 %reduce-scatter.2.cloned.1.call-done = bf16[128,8192]{1,0:T(8,128)(2,1)} async-done(((bf16[512,8192]{1,0:T(8,128)(2,1)}), bf16[128,8192]{1,0:T(8,128)(2,1)}) %reduce-scatter.2.cloned.1.call-update) | async-done | bytes 2097168 | tf_op jit(solution)/shard_map/reduce_scatter | solution.py:40
  143.9 4.0 %fusion.12 = bf16[128,8192]{1,0:T(8,128)(2,1)} fusion(bf16[128,8192]{1,0:T(8,128)(2,1)} %reduce-scatter.2.cloned.1.call-done), kind=kLoop, calls=%fused_computation.15 | loop fusion | flops 6291456 | bytes 4194304 | tf_op jit(solution)/shard_map/convert_element_type | solution.py:46
  148.0 3.3 reshape.92
  151.3 4.4 %fusion.24 = (bf16[128,1,2048]{2,1,0:T(2,128)(2,1)S(1)}, bf16[128,1,2048]{2,1,0:T(2,128)(2,1)}, f32[128,1,2048]{2,1,0:T(1,128)}, bf16[128,1,2048]{2,1,0:T(2,128)(2,1)}) fusion(bf16[128,4,2048]{2,1,0:T(4,128)(2,1)S(1)} %reshape.92), kind=kLoop, calls=%fused_computation.42 | loop fusion | flops 262144 | bytes 4718592 | tf_op jit(solution)/shard_map/slice | solution.py:49
  155.7 2.5 copy.27
  158.2 2.4 copy.26
  160.6 0.0 copy-start
  160.7 0.2 fusion.14
  160.8 0.6 copy-done
  161.5 0.1 mul.90
  161.5 1.3 copy.21
  162.9 0.4 copy_convert_fusion
  163.2 0.3 copy.22
  163.6 40.2 %all-gather.4.cloned.1.call-done = bf16[2048,2048]{0,1:T(8,128)(2,1)} async-done(((bf16[512,2048]{0,1:T(8,128)(2,1)}), bf16[2048,2048]{0,1:T(8,128)(2,1)}) %all-gather.4.cloned.1.call-update) | async-done | bytes 8388624 | tf_op jit(solution)/shard_map/all_gather | solution.py:54
  203.8 11.9 %fusion.23 = (f32[128]{0:T(128)S(1)}, f32[16,128,128]{1,2,0:T(8,128)S(1)}) fusion(f32[128,16,128]{0,2,1:T(8,128)S(1)} %bitcast.61, f32[128,16]{0,1:T(8,128)S(1)} %divide_multiply_fusion, f32[128]{0:T(128)S(1)} %get-tuple-element.5, bf16[2048,16,128]{0,2,1:T(8,128)(2,1)} %bitcast.60, pred[128,2048]{1,0:T(8,128)(4,1)S(1)} %fusion.19, ...), kind=kOutput, calls=%fused_computation.41 | convolution fusion | flops 2177892352 | bytes 19670016 | tf_op jit(solution)/shard_map/rhl,lhe->rhe/dot_general | solution.py:22
  215.7 1.3 copy.18
  217.1 11.6 %psum.21 = f32[128]{0:T(128)S(1)} all-reduce(f32[128]{0:T(128)S(1)} %get-tuple-element.12), channel_id=1, replica_groups=mesh['groups'=2,'head'=4,'hist'=4] {'head'}, use_global_device_ids=true, to_apply=%region_3.4 | all-reduce | flops 128 | bytes 1024 | tf_op jit(solution)/shard_map/psum | solution.py:66
  228.7 0.3 multiply_reduce_fusion
  229.0 8.4 %psum.22 = f32[128]{0:T(128)S(1)} all-reduce(f32[128]{0:T(128)S(1)} %multiply_reduce_fusion), channel_id=1, replica_groups=mesh['groups'=2,'head'=4,'hist'=4] {'head'}, use_global_device_ids=true, to_apply=%region_5.6 | all-reduce | flops 128 | bytes 1024 | tf_op jit(solution)/shard_map/psum | solution.py:68
  237.4 3.7 %fusion.13 = bf16[128,2048]{1,0:T(8,128)(2,1)} fusion(f32[128,1,2048]{2,1,0:T(1,128)} %get-tuple-element.10, f32[128,2048]{1,0:T(8,128)} %copy.21, f32[128,2048]{1,0:T(8,128)} %copy.18, f32[128]{0:T(128)S(1)} %add_rsqrt_fusion, f32[128]{0:T(128)S(1)} %broadcast_multiply_fusion, f32[128]{0:T(128)S(1)} %get-tuple-element.5, ...), kind=kLoop, calls=%fused_computation.19 | loop fusion | flops 2097152 | bytes 4195840 | tf_op jit(solution)/shard_map/convert_element_type | solution.py:70
  241.1 0.0 all-gather.8.cloned.1.call-update
  241.1 0.3 all-reduce.2.cloned.1.call-start
  241.4 21.1 %all-gather.8.cloned.1.call-done = bf16[512,2048]{1,0:T(8,128)(2,1)} async-done(((bf16[128,2048]{1,0:T(8,128)(2,1)}), bf16[512,2048]{1,0:T(8,128)(2,1)}) %all-gather.8.cloned.1.call-update) | async-done | bytes 2097168 | tf_op jit(solution)/shard_map/all_gather | solution.py:71
  262.5 9.9 %convolution_convert_fusion.1 = bf16[512,2048]{1,0:T(8,128)(2,1)} fusion(bf16[512,2048]{1,0:T(8,128)(2,1)} %all-gather.8.cloned.1.call-done, bf16[2048,2048]{1,0:T(8,128)(2,1)} %param.11), kind=kOutput, calls=%fused_computation.16 | convolution fusion | flops 4296015872 | bytes 12582912 | tf_op jit(solution)/shard_map/dot_general | solution.py:74
  272.4 0.0 all-reduce.2.cloned.1.call-update
  272.4 86.3 %all-reduce.2.cloned.1.call-done = bf16[512,2048]{1,0:T(8,128)(2,1)} async-done(((bf16[512,2048]{1,0:T(8,128)(2,1)}), bf16[512,2048]{1,0:T(8,128)(2,1)}) %all-reduce.2.cloned.1.call-update) | async-done | bytes 2097168 | tf_op jit(solution)/shard_map/psum | solution.py:75
  358.7 2.1 add_convert_fusion
  (3 shorter events, 0.0 us)
Async XLA Ops:
  6.5 63.4 %all-gather.6.cloned.1.call-start = ((), (), s32[]{:S(2)}) async-start(), calls=%async_computation.3 | async-start | bytes 10485760 | tf_op jit(solution)/shard_map/all_gather | solution.py:55
  7.3 136.7 %reduce-scatter.2.cloned.1.call-start = ((), (), s32[]{:S(2)}) async-start(), calls=%async_computation.1 | async-start | bytes 10485760 | tf_op jit(solution)/shard_map/reduce_scatter | solution.py:40
  7.3 30.2 %copy-start.2 = (bf16[512,2048]{1,0:T(8,128)(2,1)S(1)}, bf16[512,2048]{1,0:T(8,128)(2,1)}, u32[]{:S(2)}) copy-start(bf16[512,2048]{1,0:T(8,128)(2,1)} %param.7) | copy-start | bytes 6291460
  63.0 1.7 copy-start.1
  63.0 140.8 %all-gather.4.cloned.1.call-start = ((), (), s32[]{:S(2)}) async-start(), calls=%async_computation.2 | async-start | bytes 10485760 | tf_op jit(solution)/shard_map/all_gather | solution.py:54
  67.3 195.3 %all-gather.8.cloned.1.call-start = ((), (), s32[]{:S(2)}) async-start(), calls=%async_computation.4 | async-start | bytes 2621440 | tf_op jit(solution)/shard_map/all_gather | solution.py:71
  160.6 0.8 copy-start
  241.1 117.6 %all-reduce.2.cloned.1.call-start = ((), (), s32[]{:S(2)}) async-start(), calls=%async_computation.5 | async-start | bytes 4194304 | tf_op jit(solution)/shard_map/psum | solution.py:75
Sparse Core Ops, SparseCore 0:
  8.9 60.9 all-gather.5
  72.5 71.4 reduce-scatter.1
  145.5 58.2 all-gather.3
  241.3 21.2 all-gather.7
  272.5 86.1 all-reduce.1
where the time goes:
time: 368 us; the launch traced here: 367 us
  waiting for transfers between devices  211 us (57%)
  local copies, waits for them, and re-layouts  58.7 us (16%)
  matrix products  47.3 us (13%)
  blocking collectives  20 us (5%)
  other arithmetic  16.3 us (4%)
  between operations  13.2 us (4%)
    psum x1, waiting for transfers between devices, local(): lax.psum(whole_out.astype(jnp.bfloat16), 'head').astype(jnp.float32)  86.3 us
    reduce_scatter x1, waiting for transfers between devices, local(): lax.psum_scatter(jnp.dot(tokens, flat_weight, preferred_element_type=jnp....  61.6 us
    all_gather x1, waiting for transfers between devices, local(): lax.all_gather(k_cache, 'hist', axis=0, tiled=True)  40.2 us
    unnamed x10, local copies, waits for them, and re-layouts  39.9 us
    dot_general x1, matrix products, local(): jnp.dot(tokens, flat_weight, preferred_element_type=jnp.float32)  25.5 us
    all_gather x1, waiting for transfers between devices, local(): gathered = lax.all_gather(gated_rows, 'hist', axis=0, tiled=True)  21.1 us
    all_gather x1, local copies, waits for them, and re-layouts, local(): lax.all_gather(v_cache, 'hist', axis=0, tiled=True)  12.4 us
    dot_general x1, matrix products, history_terms(): jnp.einsum('rhl,lhe->rhe', weights, value_heads, preferred_element_type=j...  11.9 us
  transfers between devices with their start and end apart: 5, of which 5 were waited for; matrix products, arithmetic and copies ran while one was open for 25% of the time, Pallas kernels for 0%

commit v1 on v0

--- a/solution.py
+++ b/solution.py
@@ -5,6 +5,18 @@
 
 DH = 128
 epsilon = 1e-05
+
+
+def gather_by_bits(x, axis, dim):
+    ways, here, turn = (lax.axis_size(axis), lax.axis_index(axis), x.shape[dim])
+    line, have = (x, 1)
+    while have < ways:
+        line = jnp.concatenate(
+            [line, lax.ppermute(line, axis, [(d, (d - have) % ways) for d in range(ways)])],
+            axis=dim,
+        )
+        have = 2 * have
+    return jnp.roll(line, here * turn, axis=dim)
 
 
 def history_terms(query_heads, key_block, value_block, vis_lo, vis_hi):
@@ -51,7 +63,7 @@
     query_heads = own_query.reshape(own_count, local_heads, DH)
     history = history_terms(
         query_heads,
-        lax.all_gather(k_cache, "hist", axis=0, tiled=True),
+        gather_by_bits(k_cache, "hist", 0),
         lax.all_gather(v_cache, "hist", axis=0, tiled=True),
         start_own,
         end_own,

time: 368 us -> 448 us (1.22)
  waiting for transfers between devices: 211 us -> 262 us
  local copies, waits for them, and re-layouts: 58.7 us -> 82.9 us
    ppermute x0 -> x2, waiting for transfers between devices: none -> 154 us  [gather_by_bits(): lax.ppermute(line, axis, [(d, (d - have) % ways) for d in range(ways)])]
    reduce_scatter x1, waiting for transfers between devices: 61.6 us -> 0.01 us  [local(): lax.psum_scatter(jnp.dot(tokens, flat_weight, preferred_element_type=jnp....]
    all_gather x1 -> x0, waiting for transfers between devices: 40.2 us -> none  [local(): lax.all_gather(k_cache, 'hist', axis=0, tiled=True)]
    unnamed x10 -> x17, local copies, waits for them, and re-layouts: 39.9 us -> 52.1 us
    dynamic_slice x0 -> x1, local copies, waits for them, and re-layouts: none -> 8.38 us  [gather_by_bits(): return jnp.roll(line, here * turn, axis=dim)]
    concatenate x0 -> x1, local copies, waits for them, and re-layouts: none -> 4.71 us  [gather_by_bits(): return jnp.roll(line, here * turn, axis=dim)]
  transfers between devices with their start and end apart: 5 -> 6, of which waited for: 5 -> 4; matrix products, arithmetic and copies ran while one was open for 25% -> 22% of each run, Pallas kernels for 0% -> 0%
where the time goes in v1:
time: 448 us; the launch traced here: 447 us
  waiting for transfers between devices  262 us (58%)
  local copies, waits for them, and re-layouts  82.9 us (19%)
  matrix products  47.6 us (11%)
  blocking collectives  20 us (4%)
  other arithmetic  18.5 us (4%)
  between operations  13.3 us (3%)
    ppermute x2, waiting for transfers between devices, gather_by_bits(): lax.ppermute(line, axis, [(d, (d - have) % ways) for d in range(ways)])  154 us
    psum x1, waiting for transfers between devices, local(): lax.psum(whole_out.astype(jnp.bfloat16), 'head').astype(jnp.float32)  86.3 us
    unnamed x17, local copies, waits for them, and re-layouts  52.1 us
    dot_general x1, matrix products, local(): jnp.dot(tokens, flat_weight, preferred_element_type=jnp.float32)  25.5 us
    all_gather x1, waiting for transfers between devices, local(): gathered = lax.all_gather(gated_rows, 'hist', axis=0, tiled=True)  21.1 us
    all_gather x1, local copies, waits for them, and re-layouts, local(): lax.all_gather(v_cache, 'hist', axis=0, tiled=True)  12.3 us
    dot_general x1, matrix products, history_terms(): jnp.einsum('rhl,lhe->rhe', weights, value_heads, preferred_element_type=j...  12.2 us
    psum x1, blocking collectives, local(): row_sum = lax.psum(jnp.sum(attended, axis=1), 'head')  11.7 us
  transfers between devices with their start and end apart: 6, of which 4 were waited for; matrix products, arithmetic and copies ran while one was open for 22% of the time, Pallas kernels for 0%

profile of v1, /device:TPU:0, one launch (start us, length us, event | category | flops | bytes accessed | tf_op | source)
XLA Modules:
  0.0 447.2 jit_solution(1965757129780877837)
XLA Ops:
  6.5 0.7 all-gather.3.cloned.1.call-update
  7.3 0.0 reduce-scatter.2.cloned.1.call-start
  7.3 0.0 copy-start.3
  7.3 30.2 %copy.35 = bf16[256,8,4,2048]{3,1,2,0:T(8,128)(2,1)} copy(bf16[256,8,4,2048]{3,2,1,0:T(4,128)(2,1)} %bitcast.58) | data formatting | bytes 67108864
  37.5 25.5 %convolution_convert_fusion = bf16[512,8192]{1,0:T(8,128)(2,1)} fusion(bf16[512,2048]{1,0:T(8,128)(2,1)S(1)} %copy-done.3, bf16[2048,8192]{1,0:T(8,128)(2,1)} %bitcast.59), kind=kOutput, calls=%fused_computation.7 | convolution fusion | flops 17184063488 | bytes 44040192 | tf_op jit(solution)/shard_map/dot_general | solution.py:53
  63.1 0.0 reduce-scatter.2.cloned.1.call-update
  63.1 0.0 all-gather.5.cloned.1.call-start
  63.1 2.9 copy.16
  66.1 2.4 collective-permute-start
  68.5 23.6 %collective-permute-done = bf16[512,2048]{0,1:T(8,128)(2,1)S(1)} collective-permute-done((bf16[512,2048]{0,1:T(8,128)(2,1)S(1)}, bf16[512,2048]{0,1:T(8,128)(2,1)S(1)}, u32[]{:S(2)}, u32[]{:S(2)}) %collective-permute-start) | collective-permute-done | bytes 2097184 | tf_op jit(solution)/shard_map/ppermute | solution.py:15
  92.0 1.3 copy-done
  93.3 2.7 pad_maximum_fusion
  96.1 0.4 collective-permute-start.1
  96.5 0.8 convert_sqrt_fusion
  97.2 1.6 constant_dynamic-update-slice_fusion.5
  98.8 0.2 fusion.19
  99.1 3.3 constant_dynamic-update-slice_fusion.4
  102.4 130.0 %collective-permute-done.1 = bf16[1024,2048]{0,1:T(8,128)(2,1)} collective-permute-done((bf16[1024,2048]{0,1:T(8,128)(2,1)}, bf16[1024,2048]{0,1:T(8,128)(2,1)}, u32[]{:S(2)}, u32[]{:S(2)}) %collective-permute-start.1) | collective-permute-done | bytes 4194336 | tf_op jit(solution)/shard_map/ppermute | solution.py:15
  232.4 4.6 %constant_dynamic-update-slice_fusion.3 = bf16[4096,2048]{0,1:T(8,128)(2,1)} fusion(bf16[4096,2048]{0,1:T(8,128)(2,1)} %constant_dynamic-update-slice_fusion.4, bf16[1024,2048]{0,1:T(8,128)(2,1)} %collective-permute-done.1), kind=kLoop, calls=%fused_computation.38 | loop fusion | bytes 8388608
  237.0 1.6 constant_dynamic-update-slice_fusion.2
  238.6 1.6 constant_dynamic-update-slice_fusion.1
  240.2 4.7 %constant_dynamic-update-slice_fusion = bf16[4096,2048]{0,1:T(8,128)(2,1)} fusion(bf16[4096,2048]{0,1:T(8,128)(2,1)} %constant_dynamic-update-slice_fusion.1, bf16[1024,2048]{0,1:T(8,128)(2,1)} %collective-permute-done.1), kind=kLoop, calls=%fused_computation.35 | loop fusion | bytes 8388608 | tf_op jit(solution)/shard_map/jit(_roll_dynamic)/concatenate | solution.py:19
  244.9 8.4 %constant_dynamic-slice_fusion = bf16[2048,2048]{0,1:T(8,128)(2,1)} fusion(bf16[4096,2048]{0,1:T(8,128)(2,1)} %constant_dynamic-update-slice_fusion, s32[]{:T(128)S(6)} %select_n.28), kind=kLoop, calls=%fused_computation.42 | loop fusion | bytes 16777220 | tf_op jit(solution)/shard_map/jit(_roll_dynamic)/dynamic_slice | solution.py:19
  253.3 12.3 %copy.21 = bf16[2048,2048]{0,1:T(8,128)(2,1)} copy(bf16[2048,2048]{1,0:T(8,128)(2,1)} %all-gather.3.cloned.1.call-done) | data formatting | bytes 16777216 | tf_op jit(solution)/shard_map/all_gather | solution.py:67
  265.6 4.0 fusion.12
  269.7 3.3 reshape.93
  273.0 4.4 fusion.24
  277.4 2.4 copy.32
  279.8 0.0 copy-start.2
  279.8 2.6 copy.33
  282.4 0.2 fusion.14
  282.6 0.4 copy_convert_fusion
  283.0 0.3 copy.27
  283.3 12.2 %fusion.23 = (f32[128]{0:T(128)S(1)}, f32[16,128,128]{1,2,0:T(8,128)S(1)}) fusion(f32[128,16,128]{0,2,1:T(8,128)S(1)} %bitcast.63, f32[128,16]{0,1:T(8,128)S(1)} %divide_multiply_fusion, f32[128]{0:T(128)S(1)} %get-tuple-element.5, bf16[2048,16,128]{0,2,1:T(8,128)(2,1)} %bitcast.61, pred[128,2048]{0,1:T(8,128)(4,1)S(1)} %fusion.19, ...), kind=kOutput, calls=%fused_computation.49 | convolution fusion | flops 2177892352 | bytes 19670016 | tf_op jit(solution)/shard_map/rhl,lhe->rhe/dot_general | solution.py:34
  295.5 11.7 %psum.21 = f32[128]{0:T(128)S(1)} all-reduce(f32[128]{0:T(128)S(1)} %get-tuple-element.12), channel_id=1, replica_groups=mesh['groups'=2,'head'=4,'hist'=4] {'head'}, use_global_device_ids=true, to_apply=%region_3.4 | all-reduce | flops 128 | bytes 1024 | tf_op jit(solution)/shard_map/psum | solution.py:78
  307.1 0.3 multiply_reduce_fusion
  307.5 8.4 %psum.22 = f32[128]{0:T(128)S(1)} all-reduce(f32[128]{0:T(128)S(1)} %multiply_reduce_fusion), channel_id=1, replica_groups=mesh['groups'=2,'head'=4,'hist'=4] {'head'}, use_global_device_ids=true, to_apply=%region_5.6 | all-reduce | flops 128 | bytes 1024 | tf_op jit(solution)/shard_map/psum | solution.py:80
  315.8 0.3 copy.23
  316.2 0.1 mul.94
  316.2 1.3 copy.26
  317.6 3.4 fusion.13
  320.9 0.0 all-gather.5.cloned.1.call-update
  321.0 0.3 all-reduce.2.cloned.1.call-start
  321.2 21.1 %all-gather.5.cloned.1.call-done = bf16[512,2048]{1,0:T(8,128)(2,1)} async-done(((bf16[128,2048]{1,0:T(8,128)(2,1)}), bf16[512,2048]{1,0:T(8,128)(2,1)}) %all-gather.5.cloned.1.call-update) | async-done | bytes 2097168 | tf_op jit(solution)/shard_map/all_gather | solution.py:83
  342.4 9.9 %convolution_convert_fusion.1 = bf16[512,2048]{1,0:T(8,128)(2,1)} fusion(bf16[512,2048]{1,0:T(8,128)(2,1)} %all-gather.5.cloned.1.call-done, bf16[2048,2048]{1,0:T(8,128)(2,1)} %param.11), kind=kOutput, calls=%fused_computation.17 | convolution fusion | flops 4296015872 | bytes 12582912 | tf_op jit(solution)/shard_map/dot_general | solution.py:86
  352.2 0.0 all-reduce.2.cloned.1.call-update
  352.3 86.3 %all-reduce.2.cloned.1.call-done = bf16[512,2048]{1,0:T(8,128)(2,1)} async-done(((bf16[512,2048]{1,0:T(8,128)(2,1)}), bf16[512,2048]{1,0:T(8,128)(2,1)}) %all-reduce.2.cloned.1.call-update) | async-done | bytes 2097168 | tf_op jit(solution)/shard_map/psum | solution.py:87
  438.6 2.1 add_convert_fusion
  (11 shorter events, 0.0 us)
Async XLA Ops:
  6.5 246.8 %all-gather.3.cloned.1.call-start = ((), (), s32[]{:S(2)}) async-start(), calls=%async_computation.2 | async-start | bytes 10485760 | tf_op jit(solution)/shard_map/all_gather | solution.py:67
  7.3 258.4 %reduce-scatter.2.cloned.1.call-start = ((), (), s32[]{:S(2)}) async-start(), calls=%async_computation.1 | async-start | bytes 10485760 | tf_op jit(solution)/shard_map/reduce_scatter | solution.py:52
  7.3 30.2 %copy-start.3 = (bf16[512,2048]{1,0:T(8,128)(2,1)S(1)}, bf16[512,2048]{1,0:T(8,128)(2,1)}, u32[]{:S(2)}) copy-start(bf16[512,2048]{1,0:T(8,128)(2,1)} %param.7) | copy-start | bytes 6291460
  63.1 279.3 %all-gather.5.cloned.1.call-start = ((), (), s32[]{:S(2)}) async-start(), calls=%async_computation.3 | async-start | bytes 2621440 | tf_op jit(solution)/shard_map/all_gather | solution.py:83
  66.1 26.0 %collective-permute-start = (bf16[512,2048]{0,1:T(8,128)(2,1)S(1)}, bf16[512,2048]{0,1:T(8,128)(2,1)S(1)}, u32[]{:S(2)}, u32[]{:S(2)}) collective-permute-start(bf16[512,2048]{0,1:T(8,128)(2,1)S(1)} %copy.16), channel_id=1, source_target_pairs={{0,3},{1,0},{2,1},{3,2},{4,7},{5,4},{6,5},{7,6},{8,11},{9,8},{10,9... | collective-permute-start | bytes 6291464 | tf_op jit(solution)/shard_map/ppermute | solution.py:15
  92.0 1.3 copy-start
  96.1 136.3 %collective-permute-start.1 = (bf16[1024,2048]{0,1:T(8,128)(2,1)}, bf16[1024,2048]{0,1:T(8,128)(2,1)}, u32[]{:S(2)}, u32[]{:S(2)}) collective-permute-start(bf16[1024,2048]{0,1:T(8,128)(2,1)} %pad_maximum_fusion), channel_id=1, source_target_pairs={{0,2},{1,3},{2,0},{3,1},{4,6},{5,7},{6,4},{7,5},{8,10},{9,11},{10,... | collective-permute-start | bytes 12582920 | tf_op jit(solution)/shard_map/ppermute | solution.py:15
  99.0 139.6 %copy-start.1 = (bf16[512,2048]{0,1:T(8,128)(2,1)S(1)}, bf16[512,2048]{0,1:T(8,128)(2,1)}, u32[]{:S(2)}) copy-start(bf16[512,2048]{0,1:T(8,128)(2,1)} %copy-done) | copy-start | bytes 6291460
  279.8 2.8 copy-start.2
  321.0 117.6 %all-reduce.2.cloned.1.call-start = ((), (), s32[]{:S(2)}) async-start(), calls=%async_computation.4 | async-start | bytes 4194304 | tf_op jit(solution)/shard_map/psum | solution.py:87
Sparse Core Ops, SparseCore 0:
  8.9 60.9 all-gather.2
  72.5 114.3 reduce-scatter.1
  321.1 21.2 all-gather.4
  352.4 86.1 all-reduce.1
